TPU v7x, 128 devices: a whole 4x4x4 slice. The times are simulated.
128 devices in a mesh: ctx: 8 (over z, core), kv: 8 (over x_hi, y), grp: 2 (over x_lo).
Axes of the slice: x: 4 (x_hi: 2, x_lo: 2; x = x_hi * 2 + x_lo), y: 4, z: 4, core: 2. Of those that a mesh axis runs over, the one named last changes fastest.
Arguments:
- queries: bfloat16 [2048, 4096], P('ctx', ('kv', 'grp')), may hold values from -6 to 6
- keys: bfloat16 [2048, 1024], P('ctx', 'kv'), may hold values from -6 to 6
- values: bfloat16 [2048, 1024], P('ctx', 'kv'), may hold values from -6 to 6
- out_grad: bfloat16 [2048, 4096], P('ctx', ('kv', 'grp')), may hold values from -0.15625 to 0.15625
Outputs:
- query_grad: bfloat16 [2048, 4096], P('ctx', ('kv', 'grp'))
- key_grad: bfloat16 [2048, 1024], P(('ctx', 'grp'), 'kv')
- value_grad: bfloat16 [2048, 1024], P(('ctx', 'grp'), 'kv')
All inputs are finite; a program needn't handle non-finite values.
Results may differ from a plain program's by a relative error of at most 0.015.
Values may be sent and summed in bfloat16 or wider, within the bound.
A program may use at most 128 MiB of HBM per device.

v0:
```python
import jax
import jax.numpy as jnp
import numpy as np
from jax import lax
from jax.sharding import PartitionSpec as P

BLOCK = 256


def carried_in(shard, axis, combine, identity, reverse):
    count, place = (lax.axis_size(axis), lax.axis_index(axis))
    everything = lax.all_gather(shard.astype(jnp.bfloat16), axis)
    start = jnp.broadcast_to(jnp.asarray(identity, shard.dtype), shard.shape)

    def turn(k, before):
        at = count - 1 - k if reverse else k
        reached = at > place if reverse else at < place
        new = combine(before, everything[at].astype(shard.dtype))
        return jnp.where(reached, new, before)

    return lax.fori_loop(0, count, turn, start)


def tables(breadth):
    first_axis, second_axis = np.triu_indices(breadth)
    weights = np.where(first_axis == second_axis, 1.0, np.sqrt(2.0)) / np.sqrt(breadth)
    pair_map = np.zeros((breadth, breadth), np.int32)
    pair_map[first_axis, second_axis] = np.arange(first_axis.size)
    pair_map[second_axis, first_axis] = np.arange(first_axis.size)
    slopes = np.where(np.eye(breadth) > 0, 2.0, np.sqrt(2.0)) / np.sqrt(breadth)
    return (first_axis, second_axis, weights, pair_map.reshape(-1), slopes)


def expand(points_t, first_axis, second_axis, weights):
    values_t = points_t.astype(jnp.float32)
    scaling = jnp.asarray(weights, jnp.float32)[:, None]
    return (values_t[first_axis] * values_t[second_axis] * scaling).astype(jnp.bfloat16)


def unpack(state_low, pair_map):
    return state_low[pair_map]


def lift(state_full, cotangent_t, points_t, slopes):
    breadth = points_t.shape[0]
    unpacked = jnp.dot(state_full, cotangent_t, preferred_element_type=jnp.float32)
    unpacked = unpacked * jnp.asarray(slopes, jnp.float32).reshape(-1, 1)
    unpacked = unpacked.reshape(breadth, breadth, cotangent_t.shape[1])
    return jnp.sum(unpacked * points_t.astype(jnp.float32)[None, :, :], axis=1)


def within_block(query_rows, key_rows, value_rows, grad_rows, breadth):
    length = key_rows.shape[0]
    causal = jnp.arange(length)[:, None] >= jnp.arange(length)[None, :]
    scores = jnp.dot(query_rows, key_rows.T, preferred_element_type=jnp.float32)
    weight_low = jnp.where(causal, scores * scores / breadth, 0.0).astype(jnp.bfloat16)
    mixing = jnp.dot(grad_rows, value_rows.T, preferred_element_type=jnp.float32)
    slope_low = jnp.where(causal, 2.0 * scores * mixing / breadth, 0.0).astype(jnp.bfloat16)
    query_part = jnp.dot(slope_low, key_rows, preferred_element_type=jnp.float32)
    key_part = jnp.dot(slope_low.T, query_rows, preferred_element_type=jnp.float32)
    value_part = jnp.dot(weight_low.T, grad_rows, preferred_element_type=jnp.float32)
    return (query_part, key_part, value_part)


def local(queries, keys, values, out_grad):
    tok_rows, breadth = keys.shape
    first_axis, second_axis, weights, pair_map, slopes = tables(breadth)
    head_count = queries.shape[1] // breadth
    blocks = tok_rows // BLOCK
    groups = lax.axis_size("grp")
    member_id = lax.axis_index("grp")
    feat_count = first_axis.size
    feat_share = feat_count // groups
    key_blocks = keys.reshape(blocks, BLOCK, breadth)
    value_blocks = values.reshape(blocks, BLOCK, breadth)
    query_blocks = queries.reshape(blocks, BLOCK, head_count, breadth)
    grad_blocks = out_grad.reshape(blocks, BLOCK, head_count, breadth)
    key_expanded = [expand(key_blocks[0].T, first_axis, second_axis, weights)]
    key_share = [
        lax.dynamic_slice_in_dim(expanded, member_id * feat_share, feat_share, 0)
        for expanded in key_expanded
    ]
    own_terms = [jnp.dot(key_share[0], value_blocks[0], preferred_element_type=jnp.float32)]
    summed_terms = sum(own_terms)
    running = carried_in(summed_terms, "ctx", jnp.add, jnp.zeros_like(summed_terms), False)
    state_list = [running.astype(jnp.bfloat16)]
    states = lax.all_gather(jnp.stack(state_list), "grp", axis=1, tiled=True)
    current = 0
    accumulated = jnp.zeros((feat_count, breadth), jnp.float32)
    for member in range(head_count):
        expanded = expand(query_blocks[current, :, member, :].T, first_axis, second_axis, weights)
        accumulated = accumulated + jnp.dot(
            expanded, grad_blocks[current, :, member, :], preferred_element_type=jnp.float32
        )
    grad_terms = [accumulated]
    stacked = jnp.stack(grad_terms)
    combined = lax.psum_scatter(
        stacked.astype(jnp.bfloat16), "grp", scatter_dimension=1, tiled=True
    ).astype(jnp.float32)
    later_sum = jnp.sum(combined, axis=0)
    later_sum = carried_in(later_sum, "ctx", jnp.add, jnp.zeros_like(later_sum), True)
    grads = [None] * blocks
    for current in reversed(range(blocks)):
        grads[current] = later_sum.astype(jnp.bfloat16)
        later_sum = later_sum + combined[current]
    current = 0
    key_rows = key_blocks[current]
    value_rows = value_blocks[current]
    state_full = unpack(states[current], pair_map)
    key_sum = jnp.zeros((BLOCK, breadth), jnp.float32)
    value_sum = jnp.zeros((BLOCK, breadth), jnp.float32)
    head_rows = []
    for member in range(head_count):
        query_rows = query_blocks[current, :, member, :]
        grad_rows = grad_blocks[current, :, member, :]
        query_part, key_part, value_part = within_block(
            query_rows, key_rows, value_rows, grad_rows, breadth
        )
        query_part = query_part + lift(state_full, grad_rows.T, query_rows.T, slopes).T
        head_rows.append(query_part.astype(jnp.bfloat16))
        key_sum = key_sum + key_part
        value_sum = value_sum + value_part
    padded = lax.dynamic_update_slice_in_dim(
        jnp.zeros((feat_count, breadth), jnp.bfloat16), grads[current], member_id * feat_share, 0
    )
    key_sum = key_sum + lift(unpack(padded, pair_map), value_rows.T, key_rows.T, slopes).T
    value_sum = value_sum + jnp.dot(
        key_share[current].T, grads[current], preferred_element_type=jnp.float32
    )
    query_out = jnp.stack(head_rows, 1)
    value_parts = [value_sum]
    query_grad = query_out.reshape(tok_rows, head_count * breadth)
    value_partial = jnp.concatenate(value_parts, 0)
    key_mine, value_mine = (
        lax.psum_scatter(
            key_sum.astype(jnp.bfloat16), "grp", scatter_dimension=0, tiled=True
        ).astype(jnp.float32),
        lax.psum_scatter(
            value_partial.astype(jnp.bfloat16), "grp", scatter_dimension=0, tiled=True
        ).astype(jnp.float32),
    )
    return (query_grad, key_mine.astype(jnp.bfloat16), value_mine.astype(jnp.bfloat16))


def solution(mesh):
    return jax.shard_map(
        local,
        mesh=mesh,
        in_specs=(P("ctx", ("kv", "grp")), P("ctx", "kv"), P("ctx", "kv"), P("ctx", ("kv", "grp"))),
        out_specs=(P("ctx", ("kv", "grp")), P(("ctx", "grp"), "kv"), P(("ctx", "grp"), "kv")),
        check_vma=False,
    )
```

profile of v0, /device:TPU:0, one launch (start us, length us, event | category | flops | bytes accessed | tf_op | source)
XLA Modules:
  0.0 409.3 jit_solution(16712111842326120709)
XLA Ops:
  10.6 20.6 %gather_fusion = f32[8256,256]{1,0:T(8,128)} fusion(f32[128,256]{1,0:T(8,128)S(1)} %convert_bitcast_fusion.2, s32[9216]{0:T(1024)S(1)} %pad_clamp_fusion.1), kind=kCustom, calls=%fused_computation | custom fusion | bytes 16941312 | tf_op jit(solution)/shard_map/gather | solution.py:37
  31.2 20.7 %gather_fusion.1 = f32[8256,256]{1,0:T(8,128)} fusion(f32[128,256]{1,0:T(8,128)S(1)} %convert_bitcast_fusion.2, s32[9216]{0:T(1024)S(1)} %pad_clamp_fusion), kind=kCustom, calls=%fused_computation.1 | custom fusion | bytes 16941312 | tf_op jit(solution)/shard_map/gather | solution.py:37
  52.0 4.4 %fusion.4 = bf16[4128,256]{1,0:T(8,128)(2,1)S(1)} fusion(f32[8256,256]{1,0:T(8,128)} %gather_fusion.1, s32[]{:T(128)S(6)} %select_n.95, f32[8256,256]{1,0:T(8,128)} %gather_fusion, f32[4128]{0:T(1024)S(1)} %dynamic-slice), kind=kLoop, calls=%fused_computation.25 | loop fusion | flops 3170304 | bytes 10584196 | tf_op jit(solution)/shard_map/convert_element_type | solution.py:37
  59.7 20.6 %gather_fusion.3 = f32[8256,256]{1,0:T(8,128)} fusion(f32[128,256]{1,0:T(8,128)S(1)} %get-tuple-element.252, s32[9216]{0:T(1024)S(1)} %pad_clamp_fusion.1), kind=kCustom, calls=%fused_computation.3 | custom fusion | bytes 16941312 | tf_op jit(solution)/shard_map/gather | solution.py:37
  80.3 20.7 %gather_fusion.4 = f32[8256,256]{1,0:T(8,128)} fusion(f32[128,256]{1,0:T(8,128)S(1)} %get-tuple-element.252, s32[9216]{0:T(1024)S(1)} %pad_clamp_fusion), kind=kCustom, calls=%fused_computation.4 | custom fusion | bytes 16941312 | tf_op jit(solution)/shard_map/gather | solution.py:37
  101.0 20.7 %gather_fusion.5 = f32[8256,256]{1,0:T(8,128)} fusion(f32[128,256]{1,0:T(8,128)S(1)} %get-tuple-element.253, s32[9216]{0:T(1024)S(1)} %pad_clamp_fusion.1), kind=kCustom, calls=%fused_computation.5 | custom fusion | bytes 16941312 | tf_op jit(solution)/shard_map/gather | solution.py:37
  121.7 20.6 %gather_fusion.6 = f32[8256,256]{1,0:T(8,128)} fusion(f32[128,256]{1,0:T(8,128)S(1)} %get-tuple-element.253, s32[9216]{0:T(1024)S(1)} %pad_clamp_fusion), kind=kCustom, calls=%fused_computation.6 | custom fusion | bytes 16941312 | tf_op jit(solution)/shard_map/gather | solution.py:37
  142.4 7.9 %fusion.2 = f32[8256,128]{1,0:T(8,128)S(1)} fusion(f32[8256,256]{1,0:T(8,128)} %gather_fusion.3, f32[8256,256]{1,0:T(8,128)} %gather_fusion.4, f32[8256]{0:T(1024)S(1)} %copy-done.12, bf16[1,256,2,128]{1,3,2,0:T(8,128)(2,1)S(1)} %bitcast.92), kind=kOutput, calls=%fused_computation.22 | convolution fusion | flops 547405824 | bytes 21237760 | tf_op jit(solution)/shard_map/dot_general | solution.py:92
  150.7 2.4 copy-done.4
  153.1 4.8 %fusion.1 = bf16[1,8256,128]{2,1,0:T(8,128)(2,1)} fusion(f32[8256,128]{1,0:T(8,128)S(1)} %fusion.2, f32[8256,256]{1,0:T(8,128)S(1)} %copy-done.3, f32[8256,256]{1,0:T(8,128)S(1)} %copy-done.4, f32[8256]{0:T(1024)S(1)} %copy-done.12, bf16[1,256,2,128]{1,3,2,0:T(8,128)(2,1)S(1)} %bitcast.93), kind=kOutput, calls=%fused_computation.18 | convolution fusion | flops 549519360 | bytes 23351296 | tf_op jit(solution)/shard_map/dot_general | solution.py:92
  158.0 19.3 %while.30 = (s32[]{:T(128)}, f32[4128,128]{1,0:T(8,128)S(1)}, s32[]{:T(128)}, bf16[8,4128,128]{2,1,0:T(8,128)(2,1)}, s32[]{:T(128)}, /*index=5*/s32[]{:T(128)}) while((s32[]{:T(128)}, f32[4128,128]{1,0:T(8,128)S(1)}, s32[]{:T(128)}, bf16[8,4128,128]{2,1,0:T(8,128)(2,1)}, s32[]{:T(128)}, /*index=5*/s32[]{:T(128)}) %tuple.94), condition=%wide.region_1.2_spmd.clone, body=%wide.region_0.1_spmd.clone.sunk | while | flops 2113540 | bytes 5283933 | solution.py:21
  158.0 2.4 add_select_fusion.4
  160.4 2.4 add_select_fusion.4
  162.8 2.4 add_select_fusion.4
  165.3 2.4 add_select_fusion.4
  167.7 2.4 add_select_fusion.4
  170.1 2.4 add_select_fusion.4
  172.5 2.4 add_select_fusion.4
  174.9 2.4 add_select_fusion.4
  178.5 16.5 %reduce-scatter.4.cloned.1.call-done = bf16[1,4128,128]{2,1,0:T(8,128)(2,1)} async-done(((bf16[1,8256,128]{2,1,0:T(8,128)(2,1)}), bf16[1,4128,128]{2,1,0:T(8,128)(2,1)}) %reduce-scatter.4.cloned.1.call-update) | async-done | bytes 1056784 | tf_op jit(solution)/shard_map/reduce_scatter | solution.py:97
  197.9 35.3 %all-gather.10.cloned.1.call-done = bf16[8256,128]{1,0:T(8,128)(2,1)} async-done(((bf16[4128,128]{1,0:T(8,128)(2,1)}), bf16[8256,128]{1,0:T(8,128)(2,1)}) %all-gather.10.cloned.1.call-update) | async-done | bytes 2113552 | tf_op jit(solution)/shard_map/all_gather | solution.py:87
  233.2 56.8 %gather_fusion.2 = bf16[16384,128]{1,0:T(8,128)(2,1)} fusion(bf16[8256,128]{1,0:T(8,128)(2,1)} %all-gather.10.cloned.1.call-done, s32[16384]{0:T(1024)S(1)} %broadcast_clamp_fusion), kind=kCustom, calls=%fused_computation.2 | custom fusion | bytes 8454144 | tf_op jit(solution)/shard_map/gather | solution.py:41
  290.0 4.9 %multiply_reduce_fusion.2 = f32[128,256]{1,0:T(8,128)S(1)} fusion(f32[128,256]{1,0:T(8,128)S(1)} %get-tuple-element.252, f32[16384]{0:T(1024)S(1)} %copy-done.7, bf16[16384,128]{1,0:T(8,128)(2,1)} %gather_fusion.2, bf16[1,256,2,128]{1,3,2,0:T(8,128)(2,1)S(1)} %bitcast.97), kind=kOutput, calls=%fused_computation.15 | convolution fusion | flops 1086291968 | bytes 4587520 | tf_op jit(solution)/shard_map/dot_general | solution.py:46
  294.9 3.8 multiply_reduce_fusion.1
  299.6 19.4 %while.31 = (s32[]{:T(128)}, f32[4128,128]{1,0:T(8,128)S(1)}, s32[]{:T(128)}, bf16[8,4128,128]{2,1,0:T(8,128)(2,1)}, s32[]{:T(128)}, /*index=5*/s32[]{:T(128)}, s32[]{:T(128)}, s32[]{:T(128)}) while((s32[]{:T(128)}, f32[4128,128]{1,0:T(8,128)S(1)}, s32[]{:T(128)}, bf16[8,4128,128]{2,1,0:T(8,128)(2,1)}, s32[]{:T(128)}, ...), condition=%wide.region_6.7_spmd.clone, body=%wide.region_5.6_spmd.clone.sunk | while | flops 2113544 | bytes 5283995 | solution.py:21
  302.0 2.4 add_select_fusion.5
  304.4 2.4 add_select_fusion.5
  316.5 2.4 add_select_fusion.5
  318.9 3.2 fusion.21
  325.1 57.4 %gather_fusion.7 = bf16[16384,128]{1,0:T(8,128)(2,1)} fusion(bf16[8256,128]{1,0:T(8,128)(2,1)S(1)} %convert_dynamic-update-slice_fusion, s32[16384]{0:T(1024)S(1)} %broadcast_clamp_fusion), kind=kCustom, calls=%fused_computation.7 | custom fusion | bytes 8454144 | tf_op jit(solution)/shard_map/gather | solution.py:41
  382.6 4.6 %multiply_reduce_fusion = f32[128,256]{1,0:T(8,128)S(1)} fusion(f32[128,256]{1,0:T(8,128)S(1)} %convert_bitcast_fusion.2, f32[16384]{0:T(1024)S(1)} %copy-done.7, bf16[16384,128]{1,0:T(8,128)(2,1)} %gather_fusion.7, bf16[256,128]{1,0:T(8,128)(2,1)S(1)} %copy-done), kind=kOutput, calls=%fused_computation.13 | convolution fusion | flops 1086291968 | bytes 4587520 | tf_op jit(solution)/shard_map/dot_general | solution.py:46
  389.2 12.6 %reduce-scatter.6.cloned.1.call-done = bf16[128,128]{1,0:T(8,128)(2,1)} async-done(((bf16[256,128]{1,0:T(8,128)(2,1)}), bf16[128,128]{1,0:T(8,128)(2,1)}) %reduce-scatter.6.cloned.1.call-update) | async-done | bytes 32784 | tf_op jit(solution)/shard_map/reduce_scatter | solution.py:135
  (79 shorter events, 28.2 us)
Async XLA Ops:
  8.0 49.8 %copy-start = (bf16[256,128]{1,0:T(8,128)(2,1)S(1)}, bf16[256,128]{1,0:T(8,128)(2,1)}, u32[]{:S(2)}) copy-start(bf16[256,128]{1,0:T(8,128)(2,1)} %param.27) | copy-start | bytes 196612
  8.0 150.0 %all-gather.8.cloned.1.call-start = ((), (), s32[]{:S(2)}) async-start(), calls=%async_computation.7 | async-start | bytes 9510912 | tf_op jit(solution)/shard_map/all_gather | solution.py:12
  31.2 20.8 %copy-start.12 = (f32[8256]{0:T(1024)S(1)}, f32[8256]{0:T(1024)}, u32[]{:S(2)}) copy-start(f32[8256]{0:T(1024)} %constant.110.clone) | copy-start | bytes 99076
  56.4 1.4 copy-start.5
  57.8 1.7 copy-start.13
  59.5 135.5 %reduce-scatter.4.cloned.1.call-start = ((), (), s32[]{:S(2)}) async-start(), calls=%async_computation.3 | async-start | bytes 3170304 | tf_op jit(solution)/shard_map/reduce_scatter | solution.py:97
  121.7 20.6 %copy-start.14 = (bf16[256,256]{1,0:T(8,128)(2,1)S(1)}, bf16[256,256]{1,0:T(8,128)(2,1)}, u32[]{:S(2)}) copy-start(bf16[256,256]{1,0:T(8,128)(2,1)} %param.28) | copy-start | bytes 393220
  142.4 8.3 %copy-start.3 = (f32[8256,256]{1,0:T(8,128)S(1)}, f32[8256,256]{1,0:T(8,128)}, u32[]{:S(2)}) copy-start(f32[8256,256]{1,0:T(8,128)} %gather_fusion.5) | copy-start | bytes 25362436
  142.4 10.7 %copy-start.4 = (f32[8256,256]{1,0:T(8,128)S(1)}, f32[8256,256]{1,0:T(8,128)}, u32[]{:S(2)}) copy-start(f32[8256,256]{1,0:T(8,128)} %gather_fusion.6) | copy-start | bytes 25362436
  157.9 75.3 %all-gather.10.cloned.1.call-start = ((), (), s32[]{:S(2)}) async-start(), calls=%async_computation.8 | async-start | bytes 3170304 | tf_op jit(solution)/shard_map/all_gather | solution.py:87
  177.3 18.0 %copy-start.6 = (bf16[256,128]{1,0:T(8,128)(2,1)S(1)}, bf16[256,128]{1,0:T(8,128)(2,1)}, u32[]{:S(2)}) copy-start(bf16[256,128]{1,0:T(8,128)(2,1)} %param.26) | copy-start | bytes 196612
  177.3 20.6 %copy-start.15 = (s32[16384]{0:T(1024)S(1)}, s32[16384]{0:T(1024)}, u32[]{:S(2)}) copy-start(s32[16384]{0:T(1024)} %constant.122) | copy-start | bytes 196612
  178.5 121.1 %all-gather.6.cloned.1.call-start = ((), (), s32[]{:S(2)}) async-start(), calls=%async_computation.4 | async-start | bytes 9510912 | tf_op jit(solution)/shard_map/all_gather | solution.py:12
  195.0 194.1 %reduce-scatter.8.cloned.1.call-start = ((), (), s32[]{:S(2)}) async-start(), calls=%async_computation.6 | async-start | bytes 98304 | tf_op jit(solution)/shard_map/reduce_scatter | solution.py:138
  197.9 92.1 %copy-start.7 = (f32[16384]{0:T(1024)S(1)}, f32[16384]{0:T(1024)}, u32[]{:S(2)}) copy-start(f32[16384]{0:T(1024)} %constant.119) | copy-start | bytes 196612
  290.0 4.9 %copy-start.2 = (bf16[16384,128]{1,0:T(8,128)(2,1)S(1)}, bf16[16384,128]{1,0:T(8,128)(2,1)}, u32[]{:S(2)}) copy-start(bf16[16384,128]{1,0:T(8,128)(2,1)} %gather_fusion.2) | copy-start | bytes 12582916
  318.9 4.1 copy-start.1
  318.9 3.2 copy-start.9
  323.0 78.7 %reduce-scatter.6.cloned.1.call-start = ((), (), s32[]{:S(2)}) async-start(), calls=%async_computation.5 | async-start | bytes 98304 | tf_op jit(solution)/shard_map/reduce_scatter | solution.py:135
  382.6 4.7 %copy-start.10 = (f32[256,128]{1,0:T(8,128)S(1)}, f32[256,128]{1,0:T(8,128)}, u32[]{:S(2)}) copy-start(f32[256,128]{1,0:T(8,128)} %fusion.28) | copy-start | bytes 393220
  382.6 5.6 %copy-start.8 = (f32[128,256]{1,0:T(8,128)S(1)}, f32[128,256]{1,0:T(8,128)}, u32[]{:S(2)}) copy-start(f32[128,256]{1,0:T(8,128)} %multiply_reduce_fusion.1) | copy-start | bytes 393220
  382.6 5.8 %copy-start.11 = (bf16[256,1,128]{0,2,1:T(8,128)(2,1)S(1)}, bf16[256,1,128]{0,2,1:T(8,128)(2,1)}, u32[]{:S(2)}) copy-start(bf16[256,1,128]{0,2,1:T(8,128)(2,1)} %fusion.20) | copy-start | bytes 196612
Sparse Core Ops, SparseCore 0:
  59.6 52.6 all-gather.7
Sparse Core Ops, SparseCore 1:
  158.0 37.0 reduce-scatter.3
  196.5 36.6 all-gather.9
  234.8 51.0 all-gather.5
  323.1 13.5 reduce-scatter.7
  388.2 13.5 reduce-scatter.5
where the time goes:
time: 410 us; the launch traced here: 409 us
  local copies, waits for them, and re-layouts  245 us (60%)
  waiting for transfers between devices  64.5 us (16%)
  other arithmetic  47.2 us (12%)
  matrix products  36 us (9%)
  between operations  16 us (4%)
    gather x2, local copies, waits for them, and re-layouts, unpack(): return state_low[pair_map]  114 us
    gather x3, local copies, waits for them, and re-layouts, expand(): values_t[second_axis]  62 us
    gather x3, local copies, waits for them, and re-layouts, expand(): values_t[first_axis] * values_t[second_axis] * scaling  62 us
    select_n x16, other arithmetic, turn(): return jnp.where(reached, new, before)  38.3 us
    all_gather x1, waiting for transfers between devices, local(): states = lax.all_gather(jnp.stack(state_list), 'grp', axis=1, tiled=True)  35.3 us
    reduce_scatter x1, waiting for transfers between devices, local(): lax.psum_scatter(stacked.astype(jnp.bfloat16), 'grp', scatter_dimension=1...  16.5 us
    dot_general x3, matrix products, lift(): jnp.dot(state_full, cotangent_t, preferred_element_type=jnp.float32)  13.3 us
    dot_general x2, matrix products, local(): jnp.dot(expanded, grad_blocks[current, :, member, :], preferred_element_t...  12.6 us
  transfers between devices with their start and end apart: 6, of which 3 were waited for; matrix products, arithmetic and copies ran while one was open for 61% of the time, Pallas kernels for 0%

commit v1 on v0

v1 whole, which is shorter than its diff:
```python
import jax
import jax.numpy as jnp
from jax import lax
from jax.experimental import pallas as pl
from jax.experimental.pallas import tpu as pltpu
from jax.sharding import PartitionSpec as P

BLOCK = 256
HEAD = 128
HALF = 128
CHIPS = 4
MESH = pl.DeviceIdType.MESH
F32 = jnp.float32
BF16 = jnp.bfloat16


def dot(a, b, contract):
    return lax.dot_general(a, b, ((contract[:1], contract[1:]), ((), ())), preferred_element_type=F32)


def tile(key_rows, value_rows, query_rows, grad_rows, masked):
    scores = dot(key_rows, query_rows, (1, 1))
    mixing = dot(value_rows, grad_rows, (1, 1))
    if masked:
        at = lax.broadcasted_iota(jnp.int32, scores.shape, 0)
        seen_by = lax.broadcasted_iota(jnp.int32, scores.shape, 1)
        scores = jnp.where(at <= seen_by, scores, 0.0)
    weight_low = (scores * scores).astype(BF16)
    slope_low = (scores * mixing).astype(BF16)
    value_part = dot(weight_low, grad_rows, (1, 0))
    key_part = dot(slope_low, query_rows, (1, 0))
    query_part = dot(slope_low, key_rows, (0, 0))
    return query_part, key_part, value_part


def kernel(
    q_hbm, k_hbm, v_hbm, g_hbm,
    query_out, key_out, value_out,
    q, k, v, g, other_q, other_g, far_k, far_v,
    query_sum, key_sum, value_sum, other_send, other_recv, side_send, side_recv, far_send, far_recv,
    load_sem, other_send_sem, other_recv_sem, far_kv_send_sem, far_kv_recv_sem,
    far_send_sem, far_recv_sem, side_send_sem, side_recv_sem, back_send_sem, back_recv_sem,
):
    ctx = lax.axis_index("ctx")
    chip, core = ctx // 2, lax.rem(ctx, 2)
    grp = lax.axis_index("grp")

    def at(chip_to, core_to, grp_to):
        return {"ctx": chip_to * 2 + core_to, "grp": grp_to}

    twin = at(chip, 1 - core, grp)
    side = at(chip, core, 1 - grp)

    loads = [
        pltpu.make_async_copy(src, dst, load_sem.at[i])
        for i, (src, dst) in enumerate(((k_hbm, k), (q_hbm, q), (v_hbm, v), (g_hbm, g)))
    ]
    for copy in loads:
        copy.start()

    barrier = pltpu.get_barrier_semaphore()
    pl.semaphore_signal(barrier, inc=1, device_id=twin, device_id_type=MESH)
    pl.semaphore_signal(barrier, inc=1, device_id=side, device_id_type=MESH)
    for step in range(1, CHIPS):
        to = lax.rem(chip + step, CHIPS)
        for grp_to in (grp, 1 - grp):
            pl.semaphore_signal(barrier, inc=1, device_id=at(to, core, grp_to), device_id_type=MESH)
    pl.semaphore_wait(barrier, 2 + 2 * (CHIPS - 1))

    def remote(src, dst, send, recv, to):
        return pltpu.make_async_remote_copy(
            src_ref=src, dst_ref=dst, send_sem=send, recv_sem=recv, device_id=to, device_id_type=MESH
        )

    def kv_copies(step):
        to = at(lax.rem(chip + step, CHIPS), core, grp)
        slot = step - 1
        return (
            remote(k_hbm, far_k.at[slot], far_kv_send_sem.at[slot, 0], far_kv_recv_sem.at[slot, 0], to),
            remote(v_hbm, far_v.at[slot], far_kv_send_sem.at[slot, 1], far_kv_recv_sem.at[slot, 1], to),
        )

    def far_copies(step):
        slot = step - 1
        return [
            remote(
                far_send.at[slot, half], far_recv.at[slot, grp], far_send_sem.at[slot, half],
                far_recv_sem.at[slot, grp], at(lax.rem(chip - step + CHIPS, CHIPS), core, half),
            )
            for half in range(2)
        ]

    for step in (1, 3, 2):
        @pl.when(chip + step < CHIPS)
        def _():
            for copy in kv_copies(step):
                copy.start()

    other_copies = (
        remote(q_hbm, other_q, other_send_sem.at[0], other_recv_sem.at[0], twin),
        remote(g_hbm, other_g, other_send_sem.at[1], other_recv_sem.at[1], twin),
    )
    for copy in other_copies:
        copy.start()
    for copy in loads:
        copy.wait()

    def columns(head):
        return slice(head * HEAD, (head + 1) * HEAD)

    key_total = jnp.zeros((BLOCK, HEAD), F32)
    value_total = jnp.zeros((BLOCK, HEAD), F32)
    for head in range(2):
        query_part, key_part, value_part = tile(
            k[...], v[...], q[:, columns(head)], g[:, columns(head)], True
        )
        query_sum[0, head] = query_part
        query_sum[1, head] = jnp.zeros_like(query_part)
        key_total += key_part
        value_total += value_part
    key_sum[...] = key_total
    value_sum[...] = value_total
    for copy in other_copies:
        copy.wait()

    @pl.when(core == 0)
    def _():
        key_more = jnp.zeros((BLOCK, HEAD), F32)
        value_more = jnp.zeros((BLOCK, HEAD), F32)
        for head in range(2):
            query_part, key_part, value_part = tile(
                k[...], v[...], other_q[:, columns(head)], other_g[:, columns(head)], False
            )
            query_sum[1, head] += query_part
            key_more += key_part
            value_more += value_part
        key_sum[...] += key_more
        value_sum[...] += value_more

    away = pl.ds(pl.multiple_of((1 - grp) * HALF, HALF), HALF)
    mine = pl.ds(pl.multiple_of(grp * HALF, HALF), HALF)
    side_send[:, columns(0)] = (key_sum[away] * (2.0 / HEAD)).astype(BF16)
    side_send[:, columns(1)] = (value_sum[away] * (1.0 / HEAD)).astype(BF16)
    side_copy = remote(side_send, side_recv, side_send_sem, side_recv_sem, side)
    side_copy.start()

    for step in range(1, CHIPS):
        slot = step - 1

        @pl.when(chip >= step)
        def _():
            for copy in kv_copies(step):
                copy.wait_recv()
            far_key = jnp.zeros((BLOCK, HEAD), F32)
            far_value = jnp.zeros((BLOCK, HEAD), F32)
            for part, (rows, grads) in enumerate(((q, g), (other_q, other_g))):
                for head in range(2):
                    query_part, key_part, value_part = tile(
                        far_k[slot], far_v[slot], rows[:, columns(head)], grads[:, columns(head)], False
                    )
                    query_sum[part, head] += query_part
                    far_key += key_part
                    far_value += value_part
            far_key = (far_key * (2.0 / HEAD)).astype(BF16)
            far_value = (far_value * (1.0 / HEAD)).astype(BF16)
            for half in range(2):
                far_send[slot, half, :, columns(0)] = far_key[half * HALF:(half + 1) * HALF]
                far_send[slot, half, :, columns(1)] = far_value[half * HALF:(half + 1) * HALF]
            for copy in far_copies(step):
                copy.start()

    for head in range(2):
        other_send[:, columns(head)] = query_sum[1, head]
    back = remote(other_send, other_recv, back_send_sem, back_recv_sem, twin)
    back.start()

    for step in range(1, CHIPS):
        @pl.when(chip + step < CHIPS)
        def _():
            for copy in kv_copies(step):
                copy.wait_send()

    back.wait()
    for head in range(2):
        query_out[:, columns(head)] = (
            (query_sum[0, head] + other_recv[:, columns(head)]) * (2.0 / HEAD)
        ).astype(BF16)

    side_copy.wait()
    key_sum[:HALF] = key_sum[mine] * (2.0 / HEAD) + side_recv[:, columns(0)].astype(F32)
    value_sum[:HALF] = value_sum[mine] * (1.0 / HEAD) + side_recv[:, columns(1)].astype(F32)

    for step in range(1, CHIPS):
        slot = step - 1

        @pl.when(chip + step < CHIPS)
        def _():
            for grp_from in range(2):
                remote(
                    far_send.at[slot, 0], far_recv.at[slot, grp_from], far_send_sem.at[slot, 0],
                    far_recv_sem.at[slot, grp_from], side,
                ).wait_recv()
                key_sum[:HALF] += far_recv[slot, grp_from, :, columns(0)].astype(F32)
                value_sum[:HALF] += far_recv[slot, grp_from, :, columns(1)].astype(F32)

    for step in range(1, CHIPS):
        @pl.when(chip >= step)
        def _():
            for copy in far_copies(step):
                copy.wait_send()
    key_out[...] = key_sum[:HALF].astype(BF16)
    value_out[...] = value_sum[:HALF].astype(BF16)


def local(queries, keys, values, out_grad):
    steps = CHIPS - 1
    dma = pltpu.SemaphoreType.DMA
    return pl.pallas_call(
        kernel,
        out_shape=(
            jax.ShapeDtypeStruct((BLOCK, 2 * HEAD), BF16),
            jax.ShapeDtypeStruct((HALF, HEAD), BF16),
            jax.ShapeDtypeStruct((HALF, HEAD), BF16),
        ),
        in_specs=[pl.BlockSpec(memory_space=pl.ANY)] * 4,
        out_specs=(pl.BlockSpec(memory_space=pltpu.VMEM),) * 3,
        scratch_shapes=[
            pltpu.VMEM((BLOCK, 2 * HEAD), BF16),
            pltpu.VMEM((BLOCK, HEAD), BF16),
            pltpu.VMEM((BLOCK, HEAD), BF16),
            pltpu.VMEM((BLOCK, 2 * HEAD), BF16),
            pltpu.VMEM((BLOCK, 2 * HEAD), BF16),
            pltpu.VMEM((BLOCK, 2 * HEAD), BF16),
            pltpu.VMEM((steps, BLOCK, HEAD), BF16),
            pltpu.VMEM((steps, BLOCK, HEAD), BF16),
            pltpu.VMEM((2, 2, BLOCK, HEAD), F32),
            pltpu.VMEM((BLOCK, HEAD), F32),
            pltpu.VMEM((BLOCK, HEAD), F32),
            pltpu.VMEM((BLOCK, 2 * HEAD), F32),
            pltpu.VMEM((BLOCK, 2 * HEAD), F32),
            pltpu.VMEM((HALF, 2 * HEAD), BF16),
            pltpu.VMEM((HALF, 2 * HEAD), BF16),
            pltpu.VMEM((steps, 2, HALF, 2 * HEAD), BF16),
            pltpu.VMEM((steps, 2, HALF, 2 * HEAD), BF16),
            dma((4,)), dma((2,)), dma((2,)), dma((steps, 2)), dma((steps, 2)),
            dma((steps, 2)), dma((steps, 2)), dma, dma, dma, dma,
        ],
        compiler_params=pltpu.CompilerParams(collective_id=0, has_side_effects=True),
    )(queries, keys, values, out_grad)


def solution(mesh):
    return jax.shard_map(
        local,
        mesh=mesh,
        in_specs=(P("ctx", ("kv", "grp")), P("ctx", "kv"), P("ctx", "kv"), P("ctx", ("kv", "grp"))),
        out_specs=(P("ctx", ("kv", "grp")), P(("ctx", "grp"), "kv"), P(("ctx", "grp"), "kv")),
        check_vma=False,
    )
```

time: 410 us -> 27.5 us (0.07)
  the two profiles are of different devices: /device:TPU:0 before, /device:TPU:1 now
where the time goes in v1:
time: 27.5 us; the launch traced here: 27.4 us
  Pallas kernels  23.7 us (86%)
  local copies, waits for them, and re-layouts  2.96 us (11%)
  between operations  0.65 us (2%)
    pallas_call x1, Pallas kernels, local(): pl.pallas_call(kernel, out_shape=(jax.ShapeDtypeStruct((BLOCK, 2 * HEAD),...  23.7 us
    unnamed x7, local copies, waits for them, and re-layouts  2.96 us

profile of v1, /device:TPU:1, one launch (start us, length us, event | category | flops | bytes accessed | tf_op | source)
XLA Modules:
  0.0 27.4 jit_solution(674440129520311636)
XLA Ops:
  0.6 23.7 %shard_map.67 = (bf16[256,256]{1,0:T(8,128)(2,1)}, bf16[128,128]{1,0:T(8,128)(2,1)}, bf16[128,128]{1,0:T(8,128)(2,1)}) custom-call(bf16[256,256]{1,0:T(8,128)(2,1)} %q_hbm.1, bf16[256,128]{1,0:T(8,128)(2,1)} %k_hbm.1, bf16[256,128]{1,0:T(8,128)(2,1)} %v_hbm.1, bf16[256,256]{1,0:T(8,128)(2,1)} %g_hbm.1), custom_call_target="tpu_custom_call" | custom-call | tf_op jit(solution)/shard_map/pallas_call | solution.py:218
  24.4 0.0 copy-start.1
  24.4 1.6 %copy.10 = bf16[256,256]{1,0:T(8,128)(2,1)} copy(bf16[256,256]{1,0:T(8,128)(2,1)} %get-tuple-element.6) | data formatting | bytes 262144
  26.0 0.0 copy-done.1
  26.0 0.0 copy-start
  26.0 0.6 %copy.11 = bf16[128,128]{1,0:T(8,128)(2,1)} copy(bf16[128,128]{1,0:T(8,128)(2,1)S(1)} %copy-done.1) | data formatting | bytes 65536
  26.6 0.2 copy-done
  26.7 0.6 %copy.12 = bf16[128,128]{1,0:T(8,128)(2,1)} copy(bf16[128,128]{1,0:T(8,128)(2,1)S(1)} %copy-done) | data formatting | bytes 65536
Async XLA Ops:
  24.4 1.6 %copy-start.1 = (bf16[128,128]{1,0:T(8,128)(2,1)S(1)}, bf16[128,128]{1,0:T(8,128)(2,1)}, u32[]{:S(2)}) copy-start(bf16[128,128]{1,0:T(8,128)(2,1)} %get-tuple-element.7) | copy-start | bytes 98308
  26.0 0.8 %copy-start = (bf16[128,128]{1,0:T(8,128)(2,1)S(1)}, bf16[128,128]{1,0:T(8,128)(2,1)}, u32[]{:S(2)}) copy-start(bf16[128,128]{1,0:T(8,128)(2,1)} %get-tuple-element.8) | copy-start | bytes 98308

commit v2 on v1

v2 whole, which is shorter than its diff:
```python
import jax
import jax.numpy as jnp
from jax import lax
from jax.experimental import pallas as pl
from jax.experimental.pallas import tpu as pltpu
from jax.sharding import PartitionSpec as P

BLOCK = 256
HEAD = 128
HALF = 128
CHIPS = 4
STEPS = CHIPS - 1
MESH = pl.DeviceIdType.MESH
F32 = jnp.float32
BF16 = jnp.bfloat16
SLOPE = 2.0 / HEAD
WEIGHT = 1.0 / HEAD


def dot(a, b, contract):
    return lax.dot_general(a, b, ((contract[:1], contract[1:]), ((), ())), preferred_element_type=F32)


def columns(head):
    return slice(head * HEAD, (head + 1) * HEAD)


def kernel(
    q_hbm, k_hbm, v_hbm, g_hbm,
    query_out, key_out, value_out,
    q, g, kv, far_kv, weights, slopes, far_slopes,
    query_sum, key_sum, value_sum, back_recv, side_send, side_recv, far_send, far_recv,
    load_sem, other_send_sem, other_recv_sem, kv_send_sem, pass_send_sem, kv_recv_sem,
    far_send_sem, far_recv_sem, side_send_sem, side_recv_sem, back_send_sem, back_recv_sem, ready_sem,
):
    ctx = lax.axis_index("ctx")
    chip, core = ctx // 2, lax.rem(ctx, 2)
    grp = lax.axis_index("grp")
    halves = (1 - grp, grp)

    def at(chip_to, core_to, grp_to):
        return {"ctx": chip_to * 2 + core_to, "grp": grp_to}

    def remote(src, dst, send, recv, to):
        return pltpu.make_async_remote_copy(
            src_ref=src, dst_ref=dst, send_sem=send, recv_sem=recv, device_id=to, device_id_type=MESH
        )

    def signal(sem, to):
        pl.semaphore_signal(sem, inc=1, device_id=to, device_id_type=MESH)

    twin = at(chip, 1 - core, grp)
    side = at(chip, core, 1 - grp)
    after = at(lax.rem(chip + 1, CHIPS), core, grp)

    loads = [
        pltpu.make_async_copy(src, dst, load_sem.at[i])
        for i, (src, dst) in enumerate((
            (k_hbm, kv.at[0]), (v_hbm, kv.at[1]),
            (q_hbm.at[:, columns(0)], q.at[pl.ds(0, BLOCK)]), (q_hbm.at[:, columns(1)], q.at[pl.ds(BLOCK, BLOCK)]),
            (g_hbm.at[:, columns(0)], g.at[pl.ds(0, BLOCK)]), (g_hbm.at[:, columns(1)], g.at[pl.ds(BLOCK, BLOCK)]),
        ))
    ]
    for copy in loads:
        copy.start()

    barrier = pltpu.get_barrier_semaphore()
    for step in range(1, CHIPS):
        @pl.when(chip + step < CHIPS)
        def _():
            for grp_to in (grp, 1 - grp):
                signal(barrier, at(chip + step, core, grp_to))
    signal(barrier, twin)
    signal(barrier, side)
    for copy in loads:
        copy.wait()
    pl.semaphore_wait(barrier, 2 + 2 * chip)

    @pl.when(chip == CHIPS - 1)
    def _():
        signal(ready_sem.at[1], at(0, core, grp))

    @pl.when(chip >= 1)
    def _():
        signal(ready_sem.at[0], at(chip - 1, core, grp))

    own, other = pl.ds(0, 2 * BLOCK), pl.ds(2 * BLOCK, 2 * BLOCK)
    swaps = (
        remote(q.at[own], q.at[other], other_send_sem.at[0], other_recv_sem.at[0], twin),
        remote(g.at[own], g.at[other], other_send_sem.at[1], other_recv_sem.at[1], twin),
    )
    for copy in swaps:
        copy.start()

    def kv_send(which, half):
        to, slot = ((after, 0), (at(CHIPS - 1, core, grp), 2))[which]
        return remote(
            kv.at[:, pl.ds(pl.multiple_of(half * HALF, HALF), HALF)], far_kv.at[slot, half],
            kv_send_sem.at[which, half], kv_recv_sem.at[slot, half], to,
        )

    def kv_pass(half):
        return remote(far_kv.at[0, half], far_kv.at[1, half], pass_send_sem.at[half], kv_recv_sem.at[1, half], after)

    def far_copy(step, half):
        slot = step - 1
        return remote(
            far_send.at[slot, half], far_recv.at[slot, grp], far_send_sem.at[slot, half],
            far_recv_sem.at[slot, grp], at(lax.rem(chip - step + CHIPS, CHIPS), core, half),
        )

    def near(rows, masked):
        scores = dot(kv[0], q[rows], (1, 1))
        mixing = dot(kv[1], g[rows], (1, 1))
        if masked:
            place = lax.broadcasted_iota(jnp.int32, (BLOCK, BLOCK), 0)
            seen_by = lax.broadcasted_iota(jnp.int32, (BLOCK, BLOCK), 1)
            seen = place <= seen_by
            scores = jnp.where(jnp.concatenate([seen, seen], 1), scores, 0.0)
        slopes[:, rows] = (scores * mixing).astype(BF16)
        low = (scores * scores).astype(BF16)
        return dot(slopes[:, rows], q[rows], (1, 0)), dot(low, g[rows], (1, 0))

    key_sum[...], value_sum[...] = near(own, True)

    @pl.when(chip < CHIPS - 1)
    def _():
        pl.semaphore_wait(ready_sem.at[0], 1)
        kv_send(0, halves[0]).start()

        @pl.when(chip < CHIPS - 2)
        def _():
            kv_send(0, halves[1]).start()

    for copy in swaps:
        copy.wait()

    @pl.when(core == 0)
    def _():
        key_part, value_part = near(other, False)
        key_sum[...] += key_part
        value_sum[...] += value_part

    @pl.when(core == 1)
    def _():
        slopes[:, other] = jnp.zeros((BLOCK, 2 * BLOCK), BF16)

    away = pl.ds(pl.multiple_of((1 - grp) * HALF, HALF), HALF)
    mine = pl.ds(pl.multiple_of(grp * HALF, HALF), HALF)
    side_send[:, columns(0)] = (key_sum[away] * SLOPE).astype(BF16)
    side_send[:, columns(1)] = (value_sum[away] * WEIGHT).astype(BF16)
    side_copy = remote(side_send, side_recv, side_send_sem, side_recv_sem, side)
    side_copy.start()

    @pl.when(chip == 0)
    def _():
        pl.semaphore_wait(ready_sem.at[1], 1)
        for half in halves:
            kv_send(1, half).start()

    query_sum[...] = dot(kv[0], slopes[...], (0, 0))

    def far(step, half, spare, passed=False):
        slot = step - 1
        remote(
            far_kv.at[slot, half], far_kv.at[slot, half], pass_send_sem.at[half], kv_recv_sem.at[slot, half], after
        ).wait_recv()
        if passed:
            kv_pass(half).start()
        scores = dot(far_kv[slot, half, 0], q[...], (1, 1))
        mixing = dot(far_kv[slot, half, 1], g[...], (1, 1))
        far_slopes[slot, half] = (scores * mixing).astype(BF16)
        weights[spare] = (scores * scores).astype(BF16)
        far_send[slot, half, :, columns(0)] = (dot(far_slopes[slot, half], q[...], (1, 0)) * SLOPE).astype(BF16)
        far_send[slot, half, :, columns(1)] = (dot(weights[spare], g[...], (1, 0)) * WEIGHT).astype(BF16)
        far_copy(step, half).start()

    def far_query(step):
        slot = step - 1
        for half in range(2):
            query_sum[...] += dot(far_kv[slot, half, 0], far_slopes[slot, half], (0, 0))

    @pl.when((chip >= 1) & (chip < CHIPS - 1))
    def _():
        far(1, halves[0], 0, True)
        far(1, halves[1], 1, True)

        @pl.when(chip == CHIPS - 2)
        def _():
            kv_send(0, halves[1]).start()
        far_query(1)

    @pl.when(chip == CHIPS - 2)
    def _():
        far(2, halves[0], 0)
        far(2, halves[1], 1)
        far_query(2)

    @pl.when(chip == CHIPS - 1)
    def _():
        for i, (step, half) in enumerate(((3, 0), (1, 0), (3, 1), (2, 0), (2, 1), (1, 1))):
            far(step, halves[half], i % 2)
        for step in (3, 2, 1):
            far_query(step)

    back = remote(query_sum.at[:, other], back_recv, back_send_sem, back_recv_sem, twin)
    back.start()
    back.wait()
    query_rows = ((query_sum[:, own] + back_recv[...]) * SLOPE).T
    for head in range(2):
        query_out[:, columns(head)] = query_rows[head * BLOCK:(head + 1) * BLOCK].astype(BF16)

    @pl.when(chip < CHIPS - 1)
    def _():
        for half in halves:
            kv_send(0, half).wait_send()

    @pl.when(chip == 0)
    def _():
        for half in halves:
            kv_send(1, half).wait_send()

    @pl.when((chip >= 1) & (chip < CHIPS - 1))
    def _():
        for half in halves:
            kv_pass(half).wait_send()

    side_copy.wait()
    key_sum[:HALF] = key_sum[mine] * SLOPE + side_recv[:, columns(0)].astype(F32)
    value_sum[:HALF] = value_sum[mine] * WEIGHT + side_recv[:, columns(1)].astype(F32)

    for step in range(1, CHIPS):
        slot = step - 1

        @pl.when(chip + step < CHIPS)
        def _():
            for grp_from in range(2):
                remote(
                    far_send.at[slot, 0], far_recv.at[slot, grp_from], far_send_sem.at[slot, 0],
                    far_recv_sem.at[slot, grp_from], side,
                ).wait_recv()
                key_sum[:HALF] += far_recv[slot, grp_from, :, columns(0)].astype(F32)
                value_sum[:HALF] += far_recv[slot, grp_from, :, columns(1)].astype(F32)

    for step in range(1, CHIPS):
        @pl.when(chip >= step)
        def _():
            for half in halves:
                far_copy(step, half).wait_send()
    key_out[...] = key_sum[:HALF].astype(BF16)
    value_out[...] = value_sum[:HALF].astype(BF16)


def finish(*refs):
    sem = refs[-1]
    copies = [pltpu.make_async_copy(refs[i], refs[3 + i], sem.at[i]) for i in range(3)]
    for copy in copies:
        copy.start()
    for copy in copies:
        copy.wait()


def local(queries, keys, values, out_grad):
    dma = pltpu.SemaphoreType.DMA
    done = pl.pallas_call(
        kernel,
        out_shape=(
            pltpu.VMEM((BLOCK, 2 * HEAD), BF16),
            pltpu.VMEM((HALF, HEAD), BF16),
            pltpu.VMEM((HALF, HEAD), BF16),
        ),
        in_specs=[pl.BlockSpec(memory_space=pl.ANY)] * 4,
        out_specs=(pl.BlockSpec(memory_space=pltpu.VMEM),) * 3,
        scratch_shapes=[
            pltpu.VMEM((4 * BLOCK, HEAD), BF16),
            pltpu.VMEM((4 * BLOCK, HEAD), BF16),
            pltpu.VMEM((2, BLOCK, HEAD), BF16),
            pltpu.VMEM((STEPS, 2, 2, HALF, HEAD), BF16),
            pltpu.VMEM((2, HALF, 4 * BLOCK), BF16),
            pltpu.VMEM((BLOCK, 4 * BLOCK), BF16),
            pltpu.VMEM((STEPS, 2, HALF, 4 * BLOCK), BF16),
            pltpu.VMEM((HEAD, 4 * BLOCK), F32),
            pltpu.VMEM((BLOCK, HEAD), F32),
            pltpu.VMEM((BLOCK, HEAD), F32),
            pltpu.VMEM((HEAD, 2 * BLOCK), F32),
            pltpu.VMEM((HALF, 2 * HEAD), BF16),
            pltpu.VMEM((HALF, 2 * HEAD), BF16),
            pltpu.VMEM((STEPS, 2, HALF, 2 * HEAD), BF16),
            pltpu.VMEM((STEPS, 2, HALF, 2 * HEAD), BF16),
            dma((6,)), dma((2,)), dma((2,)), dma((2, 2)), dma((2,)), dma((STEPS, 2)),
            dma((STEPS, 2)), dma((STEPS, 2)), dma, dma, dma, dma,
            pltpu.SemaphoreType.REGULAR((2,)),
        ],
        compiler_params=pltpu.CompilerParams(collective_id=0, has_side_effects=True),
    )(queries, keys, values, out_grad)
    return pl.pallas_call(
        finish,
        out_shape=tuple(jax.ShapeDtypeStruct(a.shape, a.dtype) for a in done),
        in_specs=[pl.BlockSpec(memory_space=pltpu.VMEM)] * 3,
        out_specs=(pl.BlockSpec(memory_space=pl.ANY),) * 3,
        scratch_shapes=[dma((3,))],
    )(*[pltpu.with_memory_space_constraint(a, pltpu.VMEM) for a in done])


def solution(mesh):
    return jax.shard_map(
        local,
        mesh=mesh,
        in_specs=(P("ctx", ("kv", "grp")), P("ctx", "kv"), P("ctx", "kv"), P("ctx", ("kv", "grp"))),
        out_specs=(P("ctx", ("kv", "grp")), P(("ctx", "grp"), "kv"), P(("ctx", "grp"), "kv")),
        check_vma=False,
    )
```

time: 27.5 us -> 19.5 us (0.71)
  the two profiles are of different devices: /device:TPU:1 before, /device:TPU:0 now
where the time goes in v2:
time: 19.5 us; the launch traced here: 19.3 us
  Pallas kernels  18.7 us (96%)
  between operations  0.64 us (3%)
    pallas_call x1, Pallas kernels, local(): pl.pallas_call(kernel, out_shape=(pltpu.VMEM((BLOCK, 2 * HEAD), BF16), pl...  18 us
    pallas_call x1, Pallas kernels, local(): pl.pallas_call(finish, out_shape=tuple((jax.ShapeDtypeStruct(a.shape, a.d...  0.7 us

profile of v2, /device:TPU:0, one launch (start us, length us, event | category | flops | bytes accessed | tf_op | source)
XLA Modules:
  0.0 19.3 jit_solution(14398957791792064601)
XLA Ops:
  0.6 18.0 %shard_map.67 = (bf16[256,256]{1,0:T(8,128)(2,1)S(1)}, bf16[128,128]{1,0:T(8,128)(2,1)S(1)}, bf16[128,128]{1,0:T(8,128)(2,1)S(1)}) custom-call(bf16[256,256]{1,0:T(8,128)(2,1)} %q_hbm.1, bf16[256,128]{1,0:T(8,128)(2,1)} %k_hbm.1, bf16[256,128]{1,0:T(8,128)(2,1)} %v_hbm.1, bf16[256,256]{1,0:T(8,128)(2,1)} %g_hbm.1), custom_call_target="tpu_custom_call" | custom-call | tf_op jit(solution)/shard_map/pallas_call | solution.py:265
  18.6 0.7 %shard_map.68 = (bf16[256,256]{1,0:T(8,128)(2,1)}, bf16[128,128]{1,0:T(8,128)(2,1)}, bf16[128,128]{1,0:T(8,128)(2,1)}) custom-call(bf16[256,256]{1,0:T(8,128)(2,1)S(1)} %get-tuple-element.6.refs_0_, bf16[128,128]{1,0:T(8,128)(2,1)S(1)} %get-tuple-element.7.refs_1_, bf16[128,128]{1,0:T(8,128)(2,1)S(1)} %get-tuple-element.8.refs_2_), custom_call_target="tpu_custom_call" | custom-call | tf_op jit(solution)/shard_map/pallas_call | solution.py:296

commit v3 on v2

v3 whole, which is shorter than its diff:
```python
import jax
import jax.numpy as jnp
from jax import lax
from jax.experimental import pallas as pl
from jax.experimental.pallas import tpu as pltpu
from jax.sharding import PartitionSpec as P

BLOCK = 256
HEAD = 128
HALF = 128
CHIPS = 4
STEPS = CHIPS - 1
MESH = pl.DeviceIdType.MESH
F32 = jnp.float32
BF16 = jnp.bfloat16
SLOPE = 2.0 / HEAD
WEIGHT = 1.0 / HEAD
RETURNS = (1, 3, 2)
ORDERS = ((), ((1, 0), None, (1, 1)), ((1, 0), (1, 1), None, (2, 0), (2, 1)), ((3, 0), (1, 0), (3, 1), (2, 0), (2, 1), (1, 1)))


def dot(a, b, contract):
    return lax.dot_general(a, b, ((contract[:1], contract[1:]), ((), ())), preferred_element_type=F32)


def columns(head):
    return slice(head * HEAD, (head + 1) * HEAD)


def kernel(
    q_hbm, k_hbm, v_hbm, g_hbm,
    query_out, key_out, value_out,
    q, g, kv, far_kv, weights, slopes, far_slopes,
    query_sum, key_sum, value_sum, back_recv, side_send, side_recv, far_send, far_recv,
    load_sem, swap_send_sem, swap_recv_sem, kv_send_sem, wrap_send_sem, pass_send_sem, kv_recv_sem,
    far_send_sem, far_recv_sem, side_send_sem, side_recv_sem, back_send_sem, back_recv_sem,
    ready_sem,
):
    ctx = lax.axis_index("ctx")
    chip, core = ctx // 2, lax.rem(ctx, 2)
    grp = lax.axis_index("grp")
    halves = (1 - grp, grp)
    first, last = chip == 0, chip == CHIPS - 1
    inner = (chip >= 1) & (chip < CHIPS - 1)

    def at(chip_to, core_to, grp_to):
        return {"ctx": chip_to * 2 + core_to, "grp": grp_to}

    def remote(src, dst, send, recv, to):
        return pltpu.make_async_remote_copy(
            src_ref=src, dst_ref=dst, send_sem=send, recv_sem=recv, device_id=to, device_id_type=MESH
        )

    def signal(sem, to):
        pl.semaphore_signal(sem, inc=1, device_id=to, device_id_type=MESH)

    twin, side = at(chip, 1 - core, grp), at(chip, core, 1 - grp)
    after = at(lax.rem(chip + 1, CHIPS), core, grp)
    wrap = at(CHIPS - 1, core, grp)

    loads = [
        pltpu.make_async_copy(src, dst, load_sem.at[i])
        for i, (src, dst) in enumerate((
            (k_hbm, kv.at[0]), (v_hbm, kv.at[1]),
            (q_hbm.at[:, columns(0)], q.at[pl.ds(0, BLOCK)]), (q_hbm.at[:, columns(1)], q.at[pl.ds(BLOCK, BLOCK)]),
            (g_hbm.at[:, columns(0)], g.at[pl.ds(0, BLOCK)]), (g_hbm.at[:, columns(1)], g.at[pl.ds(BLOCK, BLOCK)]),
        ))
    ]
    for copy in loads:
        copy.start()

    barrier = pltpu.get_barrier_semaphore()

    @pl.when(chip >= 1)
    def _():
        signal(barrier, at(chip - 1, core, grp))

    @pl.when(chip < CHIPS - 1)
    def _():
        signal(barrier, at(chip + 1, core, grp))

    @pl.when(first)
    def _():
        signal(barrier, wrap)
    signal(barrier, side)
    signal(barrier, twin)
    pl.semaphore_wait(barrier, jnp.where(first, 3, 4))

    @pl.when(last)
    def _():
        signal(ready_sem, at(0, core, grp))

    own, other = pl.ds(0, 2 * BLOCK), pl.ds(2 * BLOCK, 2 * BLOCK)
    swaps = (
        remote(q.at[own], q.at[other], swap_send_sem.at[0], swap_recv_sem.at[0], twin),
        remote(g.at[own], g.at[other], swap_send_sem.at[1], swap_recv_sem.at[1], twin),
    )
    side_copy = remote(side_send, side_recv, side_send_sem, side_recv_sem, side)

    def kv_rows(half):
        return kv.at[:, pl.ds(pl.multiple_of(half * HALF, HALF), HALF)]

    def kv_send(half):
        return remote(kv_rows(half), far_kv.at[0, half], kv_send_sem.at[half], kv_recv_sem.at[0, half], after)

    def kv_wrap(half):
        return remote(kv_rows(half), far_kv.at[2, half], wrap_send_sem.at[half], kv_recv_sem.at[2, half], wrap)

    def kv_pass(half):
        return remote(far_kv.at[0, half], far_kv.at[1, half], pass_send_sem.at[half], kv_recv_sem.at[1, half], after)

    def far_copy(step, half):
        slot = step - 1
        return remote(
            far_send.at[slot, half], far_recv.at[slot, grp], far_send_sem.at[slot, half],
            far_recv_sem.at[slot, grp], at(lax.rem(chip + CHIPS - step, CHIPS), core, half),
        )

    def near(rows, masked):
        scores = dot(kv[0], q[rows], (1, 1))
        mixing = dot(kv[1], g[rows], (1, 1))
        if masked:
            place = lax.broadcasted_iota(jnp.int32, (BLOCK, BLOCK), 0)
            seen_by = lax.broadcasted_iota(jnp.int32, (BLOCK, BLOCK), 1)
            seen = place <= seen_by
            scores = jnp.where(jnp.concatenate([seen, seen], 1), scores, 0.0)
        slopes[:, rows] = (scores * mixing).astype(BF16)
        low = (scores * scores).astype(BF16)
        return dot(slopes[:, rows], q[rows], (1, 0)), dot(low, g[rows], (1, 0))

    away = pl.ds(pl.multiple_of((1 - grp) * HALF, HALF), HALF)
    mine = pl.ds(pl.multiple_of(grp * HALF, HALF), HALF)

    def near_rest():
        @pl.when(core == 0)
        def _():
            key_part, value_part = near(other, False)
            key_sum[...] += key_part
            value_sum[...] += value_part

        @pl.when(core == 1)
        def _():
            slopes[:, other] = jnp.zeros((BLOCK, 2 * BLOCK), BF16)

        side_send[:, columns(0)] = (key_sum[away] * SLOPE).astype(BF16)
        side_send[:, columns(1)] = (value_sum[away] * WEIGHT).astype(BF16)
        side_copy.start()

    def far(step, half, spare, passing):
        slot = step - 1
        kv_arrival(slot, half).wait_recv()
        if passing:
            kv_pass(half).start()
        scores = dot(far_kv[slot, half, 0], q[...], (1, 1))
        mixing = dot(far_kv[slot, half, 1], g[...], (1, 1))
        far_slopes[slot, half] = (scores * mixing).astype(BF16)
        weights[spare] = (scores * scores).astype(BF16)
        far_send[slot, half, :, columns(0)] = (dot(far_slopes[slot, half], q[...], (1, 0)) * SLOPE).astype(BF16)
        far_send[slot, half, :, columns(1)] = (dot(weights[spare], g[...], (1, 0)) * WEIGHT).astype(BF16)
        far_copy(step, half).start()

    def kv_arrival(slot, half):
        return remote(
            far_kv.at[slot, half], far_kv.at[slot, half], pass_send_sem.at[half], kv_recv_sem.at[slot, half], after
        )

    def far_query(step):
        slot = step - 1
        for half in range(2):
            query_sum[...] += dot(far_kv[slot, half, 0], far_slopes[slot, half], (0, 0))

    for copy in loads:
        copy.wait()

    @pl.when(chip < CHIPS - 1)
    def _():
        kv_send(halves[0]).start()

    @pl.when(first)
    def _():
        kv_send(halves[1]).start()
    for copy in swaps:
        copy.start()
    key_sum[...], value_sum[...] = near(own, True)
    for copy in swaps:
        copy.wait()

    @pl.when(first)
    def _():
        near_rest()
        pl.semaphore_wait(ready_sem, 1)
        for half in halves:
            kv_wrap(half).start()
        query_sum[...] = dot(kv[0], slopes[...], (0, 0))

    for chip_at, order in enumerate(ORDERS):
        @pl.when(chip == chip_at)
        def _():
            for i, what in enumerate(order):
                if what is None:
                    kv_send(halves[1]).start()
                else:
                    far(what[0], halves[what[1]], i % 2, what[0] == 1 and chip_at < CHIPS - 1)

    @pl.when(chip >= 1)
    def _():
        near_rest()
        query_sum[...] = dot(kv[0], slopes[...], (0, 0))
        far_query(1)

        @pl.when(chip >= 2)
        def _():
            far_query(2)

        @pl.when(last)
        def _():
            far_query(3)

    back = remote(query_sum.at[:, other], back_recv, back_send_sem, back_recv_sem, twin)
    back.start()

    back.wait()
    query_rows = ((query_sum[:, own] + back_recv[...]) * SLOPE).T
    for head in range(2):
        query_out[:, columns(head)] = query_rows[head * BLOCK:(head + 1) * BLOCK].astype(BF16)

    side_copy.wait()
    key_sum[:HALF] = key_sum[mine] * SLOPE + side_recv[:, columns(0)].astype(F32)
    value_sum[:HALF] = value_sum[mine] * WEIGHT + side_recv[:, columns(1)].astype(F32)

    @pl.when(chip < CHIPS - 1)
    def _():
        for half in halves:
            kv_send(half).wait_send()

    @pl.when(first)
    def _():
        for half in halves:
            kv_wrap(half).wait_send()

    @pl.when(inner)
    def _():
        for half in halves:
            kv_pass(half).wait_send()

    for step in RETURNS:
        slot = step - 1

        @pl.when(chip + step < CHIPS)
        def _():
            for grp_from in range(2):
                far_in = remote(
                    far_send.at[slot, 0], far_recv.at[slot, grp_from], far_send_sem.at[slot, 0],
                    far_recv_sem.at[slot, grp_from], after,
                )
                far_in.wait_recv()
                key_sum[:HALF] += far_recv[slot, grp_from, :, columns(0)].astype(F32)
                value_sum[:HALF] += far_recv[slot, grp_from, :, columns(1)].astype(F32)

    for step in range(1, CHIPS):
        @pl.when(chip >= step)
        def _():
            for half in halves:
                far_copy(step, half).wait_send()
    key_out[...] = key_sum[:HALF].astype(BF16)
    value_out[...] = value_sum[:HALF].astype(BF16)


def finish(*refs):
    sem = refs[-1]
    copies = [pltpu.make_async_copy(refs[i], refs[3 + i], sem.at[i]) for i in range(3)]
    for copy in copies:
        copy.start()
    for copy in copies:
        copy.wait()


def local(queries, keys, values, out_grad):
    dma = pltpu.SemaphoreType.DMA
    done = pl.pallas_call(
        kernel,
        out_shape=(
            pltpu.VMEM((BLOCK, 2 * HEAD), BF16),
            pltpu.VMEM((HALF, HEAD), BF16),
            pltpu.VMEM((HALF, HEAD), BF16),
        ),
        in_specs=[pl.BlockSpec(memory_space=pl.ANY)] * 4,
        out_specs=(pl.BlockSpec(memory_space=pltpu.VMEM),) * 3,
        scratch_shapes=[
            pltpu.VMEM((4 * BLOCK, HEAD), BF16),
            pltpu.VMEM((4 * BLOCK, HEAD), BF16),
            pltpu.VMEM((2, BLOCK, HEAD), BF16),
            pltpu.VMEM((STEPS, 2, 2, HALF, HEAD), BF16),
            pltpu.VMEM((2, HALF, 4 * BLOCK), BF16),
            pltpu.VMEM((BLOCK, 4 * BLOCK), BF16),
            pltpu.VMEM((STEPS, 2, HALF, 4 * BLOCK), BF16),
            pltpu.VMEM((HEAD, 4 * BLOCK), F32),
            pltpu.VMEM((BLOCK, HEAD), F32),
            pltpu.VMEM((BLOCK, HEAD), F32),
            pltpu.VMEM((HEAD, 2 * BLOCK), F32),
            pltpu.VMEM((HALF, 2 * HEAD), BF16),
            pltpu.VMEM((HALF, 2 * HEAD), BF16),
            pltpu.VMEM((STEPS, 2, HALF, 2 * HEAD), BF16),
            pltpu.VMEM((STEPS, 2, HALF, 2 * HEAD), BF16),
            dma((6,)), dma((2,)), dma((2,)), dma((2,)), dma((2,)), dma((2,)), dma((STEPS, 2)),
            dma((STEPS, 2)), dma((STEPS, 2)), dma, dma, dma, dma,
            pltpu.SemaphoreType.REGULAR,
        ],
        compiler_params=pltpu.CompilerParams(collective_id=0, has_side_effects=True),
    )(queries, keys, values, out_grad)
    return pl.pallas_call(
        finish,
        out_shape=tuple(jax.ShapeDtypeStruct(a.shape, a.dtype) for a in done),
        in_specs=[pl.BlockSpec(memory_space=pltpu.VMEM)] * 3,
        out_specs=(pl.BlockSpec(memory_space=pl.ANY),) * 3,
        scratch_shapes=[dma((3,))],
    )(*[pltpu.with_memory_space_constraint(a, pltpu.VMEM) for a in done])


def solution(mesh):
    return jax.shard_map(
        local,
        mesh=mesh,
        in_specs=(P("ctx", ("kv", "grp")), P("ctx", "kv"), P("ctx", "kv"), P("ctx", ("kv", "grp"))),
        out_specs=(P("ctx", ("kv", "grp")), P(("ctx", "grp"), "kv"), P(("ctx", "grp"), "kv")),
        check_vma=False,
    )
```

time: 19.5 us -> 18.9 us (0.969)
  Pallas kernels: 18.7 us -> 18.2 us
    pallas_call x1, Pallas kernels: 18 us -> 17.5 us  [local(): pl.pallas_call(kernel, out_shape=(pltpu.VMEM((BLOCK, 2 * HEAD), BF16), pl...]
where the time goes in v3:
time: 18.9 us; the launch traced here: 18.8 us
  Pallas kernels  18.2 us (96%)
  between operations  0.64 us (3%)
    pallas_call x1, Pallas kernels, local(): pl.pallas_call(kernel, out_shape=(pltpu.VMEM((BLOCK, 2 * HEAD), BF16), pl...  17.5 us
    pallas_call x1, Pallas kernels, local(): pl.pallas_call(finish, out_shape=tuple((jax.ShapeDtypeStruct(a.shape, a.d...  0.7 us

profile of v3, /device:TPU:0, one launch (start us, length us, event | category | flops | bytes accessed | tf_op | source)
XLA Modules:
  0.0 18.8 jit_solution(10374659369202102496)
XLA Ops:
  0.6 17.5 %shard_map.67 = (bf16[256,256]{1,0:T(8,128)(2,1)S(1)}, bf16[128,128]{1,0:T(8,128)(2,1)S(1)}, bf16[128,128]{1,0:T(8,128)(2,1)S(1)}) custom-call(bf16[256,256]{1,0:T(8,128)(2,1)} %q_hbm.1, bf16[256,128]{1,0:T(8,128)(2,1)} %k_hbm.1, bf16[256,128]{1,0:T(8,128)(2,1)} %v_hbm.1, bf16[256,256]{1,0:T(8,128)(2,1)} %g_hbm.1), custom_call_target="tpu_custom_call" | custom-call | tf_op jit(solution)/shard_map/pallas_call | solution.py:280
  18.1 0.7 %shard_map.68 = (bf16[256,256]{1,0:T(8,128)(2,1)}, bf16[128,128]{1,0:T(8,128)(2,1)}, bf16[128,128]{1,0:T(8,128)(2,1)}) custom-call(bf16[256,256]{1,0:T(8,128)(2,1)S(1)} %get-tuple-element.6.refs_0_, bf16[128,128]{1,0:T(8,128)(2,1)S(1)} %get-tuple-element.7.refs_1_, bf16[128,128]{1,0:T(8,128)(2,1)S(1)} %get-tuple-element.8.refs_2_), custom_call_target="tpu_custom_call" | custom-call | tf_op jit(solution)/shard_map/pallas_call | solution.py:311

commit v4 on v3

--- a/solution.py
+++ b/solution.py
@@ -15,7 +15,6 @@
 BF16 = jnp.bfloat16
 SLOPE = 2.0 / HEAD
 WEIGHT = 1.0 / HEAD
-RETURNS = (1, 3, 2)
 ORDERS = ((), ((1, 0), None, (1, 1)), ((1, 0), (1, 1), None, (2, 0), (2, 1)), ((3, 0), (1, 0), (3, 1), (2, 0), (2, 1), (1, 1)))
 
 
@@ -243,27 +242,44 @@
         for half in halves:
             kv_pass(half).wait_send()
 
-    for step in RETURNS:
+    def returned(step):
         slot = step - 1
-
-        @pl.when(chip + step < CHIPS)
-        def _():
-            for grp_from in range(2):
-                far_in = remote(
-                    far_send.at[slot, 0], far_recv.at[slot, grp_from], far_send_sem.at[slot, 0],
-                    far_recv_sem.at[slot, grp_from], after,
-                )
-                far_in.wait_recv()
-                key_sum[:HALF] += far_recv[slot, grp_from, :, columns(0)].astype(F32)
-                value_sum[:HALF] += far_recv[slot, grp_from, :, columns(1)].astype(F32)
-
-    for step in range(1, CHIPS):
+        for grp_from in range(2):
+            far_in = remote(
+                far_send.at[slot, 0], far_recv.at[slot, grp_from], far_send_sem.at[slot, 0],
+                far_recv_sem.at[slot, grp_from], side,
+            )
+            far_in.wait_recv()
+        both = far_recv[slot, 0].astype(F32) + far_recv[slot, 1].astype(F32)
+        return key_sum[:HALF] + both[:, columns(0)], value_sum[:HALF] + both[:, columns(1)]
+
+    def give(key_total, value_total):
+        key_out[...] = key_total.astype(BF16)
+        value_out[...] = value_total.astype(BF16)
+
+    for step in range(2, CHIPS):
         @pl.when(chip >= step)
         def _():
             for half in halves:
                 far_copy(step, half).wait_send()
-    key_out[...] = key_sum[:HALF].astype(BF16)
-    value_out[...] = value_sum[:HALF].astype(BF16)
+
+    for step in (1, 3):
+        @pl.when(chip + step < CHIPS)
+        def _():
+            key_sum[:HALF], value_sum[:HALF] = returned(step)
+
+    @pl.when(chip >= 1)
+    def _():
+        for half in halves:
+            far_copy(1, half).wait_send()
+
+    @pl.when(chip < CHIPS - 2)
+    def _():
+        give(*returned(2))
+
+    @pl.when(chip >= CHIPS - 2)
+    def _():
+        give(key_sum[:HALF], value_sum[:HALF])
 
 
 def finish(*refs):

time: 18.9 us -> 18.9 us (level)
  no operation moved by 1% of the time
where the time goes in v4:
time: 18.9 us; the launch traced here: 18.8 us
  Pallas kernels  18.1 us (96%)
  between operations  0.64 us (3%)
    pallas_call x1, Pallas kernels, local(): pl.pallas_call(kernel, out_shape=(pltpu.VMEM((BLOCK, 2 * HEAD), BF16), pl...  17.4 us
    pallas_call x1, Pallas kernels, local(): pl.pallas_call(finish, out_shape=tuple((jax.ShapeDtypeStruct(a.shape, a.d...  0.7 us

profile of v4, /device:TPU:0, one launch (start us, length us, event | category | flops | bytes accessed | tf_op | source)
XLA Modules:
  0.0 18.8 jit_solution(2106975544794055812)
XLA Ops:
  0.6 17.4 %shard_map.67 = (bf16[256,256]{1,0:T(8,128)(2,1)S(1)}, bf16[128,128]{1,0:T(8,128)(2,1)S(1)}, bf16[128,128]{1,0:T(8,128)(2,1)S(1)}) custom-call(bf16[256,256]{1,0:T(8,128)(2,1)} %q_hbm.1, bf16[256,128]{1,0:T(8,128)(2,1)} %k_hbm.1, bf16[256,128]{1,0:T(8,128)(2,1)} %v_hbm.1, bf16[256,256]{1,0:T(8,128)(2,1)} %g_hbm.1), custom_call_target="tpu_custom_call" | custom-call | tf_op jit(solution)/shard_map/pallas_call | solution.py:296
  18.1 0.7 %shard_map.68 = (bf16[256,256]{1,0:T(8,128)(2,1)}, bf16[128,128]{1,0:T(8,128)(2,1)}, bf16[128,128]{1,0:T(8,128)(2,1)}) custom-call(bf16[256,256]{1,0:T(8,128)(2,1)S(1)} %get-tuple-element.6.refs_0_, bf16[128,128]{1,0:T(8,128)(2,1)S(1)} %get-tuple-element.7.refs_1_, bf16[128,128]{1,0:T(8,128)(2,1)S(1)} %get-tuple-element.8.refs_2_), custom_call_target="tpu_custom_call" | custom-call | tf_op jit(solution)/shard_map/pallas_call | solution.py:327
